TPU v7x, 32 devices: a whole 2x2x4 slice. The times are simulated.
32 devices in a mesh: groups: 2 (over y), lat: 8 (over z, x), lon: 2 (over core).
Axes of the slice: x: 2, y: 2, z: 4, core: 2. Of those that a mesh axis runs over, the one named last changes fastest.
Arguments:
- tokens: bfloat16 [16, 256, 768], P(('groups', 'lat'), 'lon'), parts along dimension 0, may hold values from -5 to 5
- gain_attn: float32 [768], replicated, may hold values from 0.25 to 1.75
- w_qkv: bfloat16 [768, 2304], P('lat'), may hold values from -0.048353085 to 0.048353085
- key_bias: bfloat16 [8, 12, 256], P('lat', None, 'lon'), may hold values from -3 to 250
- w_out: bfloat16 [768, 768], P('lat'), may hold values from -0.21875 to 0.21875
- gain_conv: float32 [768], replicated, may hold values from 0.25 to 1.75
- w_conv: bfloat16 [2, 768, 64], replicated, may hold values from -0.75 to 0.75
- lat_taps: float32 [16, 2], replicated, may hold values from -2 to 2
- lon_half: int32 [8], P('lat'), may hold values from 1 to 128, as said below
- lat_half: int32 [8], P('lat'), may hold values from 0 to 1, as said below
- quad_off: int32 [8], P('lat'), may hold values from 0 to 13
Outputs:
- updated: bfloat16 [16, 256, 768], P(('groups', 'lat'), 'lon'), parts along dimension 0
There are 2 independent parts, one for each index of `groups`. A program takes and returns all parts, laid end to end along the dimension named above; an argument that names none is the same for every part. Nothing has to cross between parts.
Inputs may be any that keep to these rules, and one draw needn't show every extreme that they name: `lon_half`: the bands at either pole reach 128. `lat_half`: both polar bands have 1.
All inputs are finite; a program needn't handle non-finite values.
Results may differ from a plain program's by a relative error of at most 0.008.
Values may be sent and summed in bfloat16 or wider, within the bound.
A program may use at most 64 MiB of HBM per device.

v0:
```python
import jax
import jax.numpy as jnp
from jax import lax
from jax.sharding import PartitionSpec as P


def padded(cells, sides, width):
    for axis, dim in sides:
        count = lax.axis_size(axis)
        ends = count - 1
        head = lax.slice_in_dim(cells, 0, width, axis=dim)
        tail = lax.slice_in_dim(cells, cells.shape[dim] - width, cells.shape[dim], axis=dim)
        cells = jnp.concatenate(
            [
                lax.ppermute(tail, axis, [(i, (i + 1) % count) for i in range(ends)]),
                cells,
                lax.ppermute(head, axis, [((i + 1) % count, i) for i in range(ends)]),
            ],
            axis=dim,
        )
    return cells


def layer_norm(inputs, gain):
    values = inputs.astype(jnp.float32)
    average = jnp.mean(values, axis=-1, keepdims=True)
    centered = values - average
    variance = jnp.mean(centered * centered, axis=-1, keepdims=True)
    return centered * lax.rsqrt(variance + 1e-05) * gain


def group_mix(inputs, w_conv):
    basis, length, channels = inputs.shape
    group_width = w_conv.shape[2]
    groups = channels // group_width
    mixed_rows = jnp.einsum(
        "kjgc,kgce->kjge",
        inputs.reshape(basis, length, groups, group_width),
        w_conv.reshape(basis, groups, group_width, group_width),
        preferred_element_type=jnp.float32,
    )
    return mixed_rows.reshape(basis, length, channels).astype(jnp.bfloat16)


def lon_weights(row_ids, col_ids, half_width, lon_total):
    offset_lon = (
        jnp.mod(col_ids[None, :] - row_ids[:, None] + lon_total // 2, lon_total) - lon_total // 2
    )
    distance = jnp.abs(offset_lon).astype(jnp.float32)
    span_plus = (half_width + 1).astype(jnp.float32)
    tent_weight = jnp.where(
        distance <= half_width.astype(jnp.float32), (1.0 - distance / span_plus) / span_plus, 0.0
    )
    odd_weight = tent_weight * offset_lon.astype(jnp.float32) / span_plus
    return jnp.stack([tent_weight, odd_weight]).astype(jnp.bfloat16)


def start_state(query_count, head_count, head_dim):
    running_max = jnp.full((head_count, query_count), -jnp.inf, jnp.float32)
    running_sum = jnp.zeros((head_count, query_count), jnp.float32)
    running_out = jnp.zeros((query_count, head_count, head_dim), jnp.float32)
    return (running_max, running_sum, running_out)


def attend_keys(carry_state, queries, key_rows, value_rows, bias_rows, score_scale):
    key_count = key_rows.shape[0]
    for offset in range(0, key_count, 128):
        running_max, running_sum, running_out = carry_state
        key_block = key_rows[offset : offset + 128]
        value_block = value_rows[offset : offset + 128]
        bias_block = bias_rows[offset : offset + 128]
        scores = (
            jnp.einsum("qhd,khd->hqk", queries, key_block, preferred_element_type=jnp.float32)
            * score_scale
        )
        scores = scores + bias_block.T.astype(jnp.float32)[:, None, :]
        new_max = jnp.maximum(running_max, jnp.max(scores, axis=-1))
        rescale = jnp.exp(running_max - new_max)
        exp_scores = jnp.exp(scores - new_max[:, :, None])
        running_sum = running_sum * rescale + jnp.sum(exp_scores, axis=-1)
        running_out = running_out * rescale.T[:, :, None] + jnp.einsum(
            "hqk,khd->qhd",
            exp_scores.astype(jnp.bfloat16),
            value_block,
            preferred_element_type=jnp.float32,
        )
        carry_state = (new_max, running_sum, running_out)
    return carry_state


def finish_state(carry_state):
    running_max, running_sum, running_out = carry_state
    finished = running_out / running_sum.T[:, :, None]
    return finished.reshape(finished.shape[0], -1).astype(jnp.bfloat16)


def lon_conv(blended, half_width, first_col, out_cols):
    lon_total = blended.shape[1]
    block_cols = min(128, lon_total)
    block_count = lon_total // block_cols
    first_block = jnp.floor_divide(first_col - half_width, block_cols)
    last_block = jnp.floor_divide(first_col + out_cols - 1 + half_width, block_cols)
    turn_count = jnp.minimum(block_count, last_block - first_block + 1)
    row_ids = first_col + jnp.arange(out_cols, dtype=jnp.int32)

    def add_block(turn_index, running_out):
        block_at = jnp.mod(first_block + turn_index, block_count)
        lon_block = lax.dynamic_slice_in_dim(blended, block_at * block_cols, block_cols, 1)
        col_ids = block_at * block_cols + jnp.arange(block_cols, dtype=jnp.int32)
        coeffs = lon_weights(row_ids, col_ids, half_width, lon_total)
        return running_out + jnp.einsum(
            "kjc,kcd->jd", coeffs, lon_block, preferred_element_type=jnp.float32
        )

    initial = jnp.zeros((out_cols, blended.shape[2]), jnp.float32)
    return lax.fori_loop(0, turn_count, add_block, initial)


def per_device(
    tokens,
    gain_attn,
    w_qkv,
    key_bias,
    w_out,
    gain_conv,
    w_conv,
    lat_taps,
    lon_half,
    lat_half,
    quad_off,
):
    own_tokens = tokens[0]
    count_lon, model_width = own_tokens.shape
    head_count = key_bias.shape[1]
    head_dim = model_width // head_count
    score_scale = head_dim ** (-0.5)
    lon_place = lax.axis_index("lon")
    normed = layer_norm(own_tokens, gain_attn).astype(jnp.bfloat16)
    bias_rows = key_bias[0].T
    full_qkv, full_out = (
        lax.all_gather(w_qkv, "lat", axis=0, tiled=True),
        lax.all_gather(w_out, "lat", axis=0, tiled=True),
    )
    projected = jnp.dot(normed, full_qkv, preferred_element_type=jnp.float32).astype(jnp.bfloat16)
    queries = projected[:, :model_width].reshape(count_lon, head_count, head_dim)
    key_here = projected[:, model_width : 2 * model_width]
    value_here = projected[:, 2 * model_width :]
    key_piece = lax.all_gather(key_here, "lon", axis=0, tiled=True)
    value_piece = lax.all_gather(value_here, "lon", axis=0, tiled=True)
    bias_piece = lax.all_gather(bias_rows, "lon", axis=0, tiled=True)
    length = key_piece.shape[0]
    carry_state = attend_keys(
        start_state(count_lon, head_count, head_dim),
        queries,
        key_piece.reshape(length, head_count, head_dim),
        value_piece.reshape(length, head_count, head_dim),
        bias_piece,
        score_scale,
    )
    attended = finish_state(carry_state)
    branch_out = jnp.dot(attended, full_out, preferred_element_type=jnp.float32)
    middle = (own_tokens.astype(jnp.float32) + branch_out).astype(jnp.bfloat16)
    conv_in = layer_norm(middle, gain_conv).astype(jnp.bfloat16)
    stacked = padded(conv_in[None], (("lat", 0),), 1)
    lat_row = lax.axis_index("lat")
    last_band = lax.axis_size("lat") - 1
    offsets = jnp.arange(3, dtype=jnp.int32) - 1
    one_hot = (
        (quad_off[0] + offsets + 1)[:, None]
        == jnp.arange(lat_taps.shape[0], dtype=jnp.int32)[None, :]
    ).astype(jnp.float32)
    tap_vals = jnp.dot(one_hot, lat_taps, precision=lax.Precision.HIGHEST)
    tap_vals = jnp.where((jnp.abs(offsets) <= lat_half[0])[:, None], tap_vals, 0.0)
    summed = jnp.einsum(
        "rk,rjd->kjd", tap_vals, stacked.astype(jnp.float32), precision=lax.Precision.HIGHEST
    ).astype(jnp.bfloat16)
    pole_gain = jnp.where(lat_row == 0, tap_vals[0], 0.0) + jnp.where(
        lat_row == last_band, tap_vals[2], 0.0
    )
    first_col = lon_place * count_lon
    pole_rows = (pole_gain[:, None, None] * conv_in.astype(jnp.float32)[None]).astype(jnp.bfloat16)
    mixed_rows = group_mix(summed, w_conv)
    pole_mixed = group_mix(pole_rows, w_conv)
    circle_rows, pole_all = (
        lax.all_gather(mixed_rows, "lon", axis=1, tiled=True),
        lax.all_gather(pole_mixed, "lon", axis=1, tiled=True),
    )
    lon_total = circle_rows.shape[1]
    blended = (
        circle_rows.astype(jnp.float32)
        + jnp.roll(pole_all, -(lon_total // 2), axis=1).astype(jnp.float32)
    ).astype(jnp.bfloat16)
    conv_out = lon_conv(blended, lon_half[0], first_col, count_lon)
    return (middle.astype(jnp.float32) + conv_out).astype(jnp.bfloat16)[None]


def solution(mesh):
    return jax.shard_map(
        per_device,
        mesh=mesh,
        in_specs=(
            P(("groups", "lat"), "lon", None),
            P(),
            P("lat", None),
            P("lat", None, "lon"),
            P("lat", None),
            P(),
            P(),
            P(),
            P("lat"),
            P("lat"),
            P("lat"),
        ),
        out_specs=P(("groups", "lat"), "lon", None),
        check_vma=False,
    )
```

profile of v0, /device:TPU:9, one launch (start us, length us, event | category | flops | bytes accessed | tf_op | source)
XLA Modules:
  0.0 145.8 jit_solution(11945221781708907703)
XLA Ops:
  6.5 0.7 all-gather.3.cloned.1.call-update
  7.3 0.0 all-gather.5.cloned.1.call-start
  7.3 0.7 all-gather.5.cloned.1.call-update
  8.7 1.0 convert_reduce_fusion
  9.7 1.1 fusion.29
  10.9 2.5 %all_gather.23 = bf16[256,12]{0,1:T(8,128)(2,1)S(1)} all-gather(bf16[128,12]{0,1:T(8,128)(2,1)} %bitcast.119), channel_id=1, replica_groups=mesh['groups'=2,'lat'=8,'lon'=2] {'lon'}, dimensions={0}, use_global_device_ids=true | all-gather | bytes 9216 | tf_op jit(solution)/shard_map/all_gather | solution.py:150
  14.7 1.3 reshape.244
  16.0 0.2 convolution_select_fusion
  16.2 0.2 add_reduce_fusion
  16.4 58.0 %all-gather.3.cloned.1.call-done = bf16[768,2304]{1,0:T(8,128)(2,1)} async-done(((bf16[96,2304]{1,0:T(8,128)(2,1)}), bf16[768,2304]{1,0:T(8,128)(2,1)}) %all-gather.3.cloned.1.call-update) | async-done | bytes 3538960 | tf_op jit(solution)/shard_map/all_gather | solution.py:141
  74.4 2.7 %convolution_convert_fusion = bf16[128,2304]{1,0:T(8,128)(2,1)S(1)} fusion(bf16[768,2304]{1,0:T(8,128)(2,1)} %all-gather.3.cloned.1.call-done, bf16[1,128,768]{2,1,0:T(8,128)(2,1)S(1)} %copy-done.1, f32[768]{0:T(1024)S(1)} %copy-done.3, f32[128]{0:T(128)S(1)} %add_rsqrt_fusion.1, f32[128]{0:T(128)S(1)} %broadcast_multiply_fusion.1), kind=kOutput, calls=%fused_computation.20 | convolution fusion | flops 453771264 | bytes 4329472 | tf_op jit(solution)/shard_map/dot_general | solution.py:144
  77.1 3.7 %all_gather.22 = bf16[256,768]{1,0:T(8,128)(2,1)S(1)} all-gather(bf16[128,768]{1,0:T(8,128)(2,1)S(1)} %get-tuple-element.186), channel_id=1, replica_groups=mesh['groups'=2,'lat'=8,'lon'=2] {'lon'}, dimensions={0}, use_global_device_ids=true | all-gather | bytes 589824 | tf_op jit(solution)/shard_map/all_gather | solution.py:148
  80.8 0.2 copy.28
  81.0 0.2 copy.27
  81.2 0.2 copy.31
  81.3 2.1 %all_gather.24 = bf16[256,768]{1,0:T(8,128)(2,1)S(1)} all-gather(bf16[128,768]{1,0:T(8,128)(2,1)S(1)} %get-tuple-element.187), channel_id=1, replica_groups=mesh['groups'=2,'lat'=8,'lon'=2] {'lon'}, dimensions={0}, use_global_device_ids=true | all-gather | bytes 589824 | tf_op jit(solution)/shard_map/all_gather | solution.py:149
  83.5 0.2 copy.29
  83.6 0.2 copy.32
  83.8 0.4 fusion.58
  84.2 0.4 fusion.59
  84.7 0.3 fusion.22
  85.0 0.2 fusion.17
  85.2 0.2 fusion.18
  85.5 30.8 %all-gather.5.cloned.1.call-done = bf16[768,768]{1,0:T(8,128)(2,1)} async-done(((bf16[96,768]{1,0:T(8,128)(2,1)}), bf16[768,768]{1,0:T(8,128)(2,1)}) %all-gather.5.cloned.1.call-update) | async-done | bytes 1179664 | tf_op jit(solution)/shard_map/all_gather | solution.py:142
  116.3 1.7 %fusion.60 = (f32[128]{0:T(128)S(1)}, f32[128,768]{1,0:T(8,128)S(1)}) fusion(bf16[128,768]{0,1:T(8,128)(2,1)S(1)} %bitcast.117, bf16[768,768]{1,0:T(8,128)(2,1)} %all-gather.5.cloned.1.call-done, bf16[1,128,768]{2,1,0:T(8,128)(2,1)S(1)} %copy-done.1), kind=kOutput, calls=%fused_computation.99 | convolution fusion | flops 151486336 | bytes 1966592 | tf_op jit(solution)/shard_map/dot_general | solution.py:161
  118.0 0.2 multiply_reduce_fusion
  118.2 0.1 fusion.51
  118.3 2.2 %collective-permute-start = (bf16[1,128,768]{2,1,0:T(8,128)(2,1)S(1)}, bf16[1,128,768]{2,1,0:T(8,128)(2,1)S(1)}, u32[]{:S(2)}, u32[]{:S(2)}) collective-permute-start(bf16[1,128,768]{2,1,0:T(8,128)(2,1)S(1)} %get-tuple-element.190), channel_id=1, source_target_pairs={{0,2},{2,4},{4,6},{6,8},{8,10},{10,12},{12,14},{1,3},{3,5},{5,7},{... | collective-permute-start | bytes 589832 | tf_op jit(solution)/shard_map/ppermute | solution.py:15
  120.5 4.0 %collective-permute-start.1 = (bf16[1,128,768]{2,1,0:T(8,128)(2,1)S(1)}, bf16[1,128,768]{2,1,0:T(8,128)(2,1)S(1)}, u32[]{:S(2)}, u32[]{:S(2)}) collective-permute-start(bf16[1,128,768]{2,1,0:T(8,128)(2,1)S(1)} %get-tuple-element.190), channel_id=1, source_target_pairs={{2,0},{4,2},{6,4},{8,6},{10,8},{12,10},{14,12},{3,1},{5,3},{7,5},{... | collective-permute-start | bytes 589832 | tf_op jit(solution)/shard_map/ppermute | solution.py:17
  124.5 0.2 copy.38
  124.7 0.3 convolution_convert_fusion.2
  125.0 0.2 copy.40
  125.2 4.1 %all_gather.27 = bf16[2,256,768]{2,1,0:T(8,128)(2,1)S(1)} all-gather(bf16[2,128,768]{2,1,0:T(8,128)(2,1)S(1)} %copy.40), channel_id=1, replica_groups=mesh['groups'=2,'lat'=8,'lon'=2] {'lon'}, dimensions={1}, use_global_device_ids=true | all-gather | bytes 1179648 | tf_op jit(solution)/shard_map/all_gather | solution.py:186
  129.3 0.1 fusion.54
  129.4 2.8 %collective-permute-done.1 = bf16[1,128,768]{2,1,0:T(8,128)(2,1)S(1)} collective-permute-done((bf16[1,128,768]{2,1,0:T(8,128)(2,1)S(1)}, bf16[1,128,768]{2,1,0:T(8,128)(2,1)S(1)}, u32[]{:S(2)}, u32[]{:S(2)}) %collective-permute-start.1) | collective-permute-done | bytes 196640 | tf_op jit(solution)/shard_map/ppermute | solution.py:17
  132.2 0.1 pad_maximum_fusion
  132.2 1.4 convolution_convert_fusion.1
  133.7 0.5 copy.35
  134.2 0.3 convolution_convert_fusion.3
  134.4 0.2 copy.37
  134.6 2.5 %all_gather.26 = bf16[2,256,768]{2,1,0:T(8,128)(2,1)S(1)} all-gather(bf16[2,128,768]{2,1,0:T(8,128)(2,1)S(1)} %copy.37), channel_id=1, replica_groups=mesh['groups'=2,'lat'=8,'lon'=2] {'lon'}, dimensions={1}, use_global_device_ids=true | all-gather | bytes 1179648 | tf_op jit(solution)/shard_map/all_gather | solution.py:185
  137.1 0.2 add_convert_fusion
  137.4 0.9 while.14
  137.4 0.1 fusion.78
  137.6 0.2 fusion.79
  137.8 0.1 fusion.78
  138.0 0.2 fusion.79
  138.3 0.7 fusion.40
  (25 shorter events, 0.2 us)
Async XLA Ops:
  6.5 9.5 %copy-start = (f32[16,2]{0,1:T(2,128)S(1)}, f32[16,2]{0,1:T(2,128)}, u32[]{:S(2)}) copy-start(f32[16,2]{0,1:T(2,128)} %param.20) | copy-start | bytes 388
  6.5 67.8 %copy-start.1 = (bf16[1,128,768]{2,1,0:T(8,128)(2,1)S(1)}, bf16[1,128,768]{2,1,0:T(8,128)(2,1)}, u32[]{:S(2)}) copy-start(bf16[1,128,768]{2,1,0:T(8,128)(2,1)} %param.13) | copy-start | bytes 589828
  6.5 67.8 %copy-start.3 = (f32[768]{0:T(1024)S(1)}, f32[768]{0:T(1024)}, u32[]{:S(2)}) copy-start(f32[768]{0:T(1024)} %param.14) | copy-start | bytes 9220
  6.5 67.8 %all-gather.3.cloned.1.call-start = ((), (), s32[]{:S(2)}) async-start(), calls=%async_computation | async-start | bytes 3981312 | tf_op jit(solution)/shard_map/all_gather | solution.py:141
  7.3 109.0 %all-gather.5.cloned.1.call-start = ((), (), s32[]{:S(2)}) async-start(), calls=%async_computation.1 | async-start | bytes 1327104 | tf_op jit(solution)/shard_map/all_gather | solution.py:142
  85.5 32.7 %copy-start.2 = (f32[768]{0:T(1024)S(1)}, f32[768]{0:T(1024)}, u32[]{:S(2)}) copy-start(f32[768]{0:T(1024)} %param.18) | copy-start | bytes 9220
  118.3 11.1 %collective-permute-start = (bf16[1,128,768]{2,1,0:T(8,128)(2,1)S(1)}, bf16[1,128,768]{2,1,0:T(8,128)(2,1)S(1)}, u32[]{:S(2)}, u32[]{:S(2)}) collective-permute-start(bf16[1,128,768]{2,1,0:T(8,128)(2,1)S(1)} %get-tuple-element.190), channel_id=1, source_target_pairs={{0,2},{2,4},{4,6},{6,8},{8,10},{10,12},{12,14},{1,3},{3,5},{5,7},{... | collective-permute-start | bytes 589832 | tf_op jit(solution)/shard_map/ppermute | solution.py:15
  120.5 11.6 %collective-permute-start.1 = (bf16[1,128,768]{2,1,0:T(8,128)(2,1)S(1)}, bf16[1,128,768]{2,1,0:T(8,128)(2,1)S(1)}, u32[]{:S(2)}, u32[]{:S(2)}) collective-permute-start(bf16[1,128,768]{2,1,0:T(8,128)(2,1)S(1)} %get-tuple-element.190), channel_id=1, source_target_pairs={{2,0},{4,2},{6,4},{8,6},{10,8},{12,10},{14,12},{3,1},{5,3},{7,5},{... | collective-permute-start | bytes 589832 | tf_op jit(solution)/shard_map/ppermute | solution.py:17
Sparse Core Ops, SparseCore 0:
  9.5 64.7 all-gather.2
  76.6 39.6 all-gather.4
where the time goes:
time: 146 us
  waiting for transfers between devices  92.9 us (64%)
  between operations  15.7 us (11%)
  blocking collectives  14.8 us (10%)
  matrix products  8.42 us (6%)
  starting transfers between devices  6.22 us (4%)
  other arithmetic  4.29 us (3%)
  local copies, waits for them, and re-layouts  3.28 us (2%)
    all_gather x1, waiting for transfers between devices, per_device(): lax.all_gather(w_qkv, 'lat', axis=0, tiled=True)  58 us
    all_gather x1, waiting for transfers between devices, per_device(): lax.all_gather(w_out, 'lat', axis=0, tiled=True)  30.8 us
    all_gather x1, blocking collectives, per_device(): lax.all_gather(pole_mixed, 'lon', axis=1, tiled=True)  4.1 us
    ppermute x1, starting transfers between devices, padded(): lax.ppermute(head, axis, [((i + 1) % count, i) for i in range(ends)])  4 us
    all_gather x1, blocking collectives, per_device(): key_piece = lax.all_gather(key_here, 'lon', axis=0, tiled=True)  3.68 us
  transfers between devices with their start and end apart: 4, of which 3 were waited for; matrix products, arithmetic and copies ran while one was open for 7% of the time, Pallas kernels for 0%

commit v1 on v0

--- a/solution.py
+++ b/solution.py
@@ -1,6 +1,8 @@
 import jax
 import jax.numpy as jnp
 from jax import lax
+from jax.experimental import pallas as pl
+from jax.experimental.pallas import tpu as pltpu
 from jax.sharding import PartitionSpec as P
 
 
@@ -194,9 +196,421 @@
     return (middle.astype(jnp.float32) + conv_out).astype(jnp.bfloat16)[None]
 
 
+BF = jnp.bfloat16
+F32 = jnp.float32
+MESH = pl.DeviceIdType.MESH
+
+
+def norm_rows(values, gain):
+    values = values.astype(F32)
+    average = jnp.mean(values, axis=-1, keepdims=True)
+    centered = values - average
+    variance = jnp.mean(centered * centered, axis=-1, keepdims=True)
+    return (centered * lax.rsqrt(variance + 1e-05) * gain).astype(BF)
+
+
+def fused_kernel(
+    nx, nz,
+    lat_taps, lon_half, lat_half, quad_off,
+    tokens, gain_attn, w_qkv, key_bias, w_out, gain_conv, w_conv,
+    out,
+    wq, wo, tok, normed, bias, bias_f, att_out, att_in, halo, other_in, mixer, mixed_all, middle,
+    q_send, q_recv, o_send, o_recv, r_send, r_recv, t_send, t_recv, a_send, a_recv, h_send, h_recv,
+):
+    y, place, c = lax.axis_index("groups"), lax.axis_index("lat"), lax.axis_index("lon")
+    z, x = lax.div(place, nx), lax.rem(place, nx)
+    quad = y * 2 + c
+    x_peer = (y, z * nx + (1 - x), c)
+    z_up, z_down = (y, place + nx, c), (y, place - nx, c)
+    sibling = (y, place, 1 - c)
+    y_peer = (1 - y, place, c)
+    diagonal = (1 - y, place, 1 - c)
+    band_up, band_down = (y, place + 1, c), (y, place - 1, c)
+    has_up, has_down = z < nz - 1, z > 0
+    cross_up = jnp.logical_and(x == 1, has_up)
+    cross_down = jnp.logical_and(x == 0, has_down)
+    lat_count = nx * nz
+    shard = w_qkv.shape[0]
+    width = tokens.shape[1]
+    rows = tokens.shape[0]
+    head = 64
+    part = width // 4
+    half = width // 2
+
+    barrier = pltpu.get_barrier_semaphore()
+
+    def greet(device):
+        pl.semaphore_signal(barrier, inc=1, device_id=device, device_id_type=MESH)
+
+    for device in (x_peer, sibling, y_peer, diagonal):
+        greet(device)
+    for cond, device in (
+        (has_up, z_up), (has_down, z_down), (cross_up, band_up), (cross_down, band_down)
+    ):
+        @pl.when(cond)
+        def _(device=device):
+            greet(device)
+
+    for pick in range(4):
+        @pl.when(quad == pick)
+        def _(pick=pick):
+            wq[pl.ds(place * shard, shard), :] = jnp.concatenate(
+                [w_qkv[:, j * width + pick * part : j * width + (pick + 1) * part] for j in range(3)],
+                axis=1,
+            )
+    tok[y, pl.ds(c * rows, rows), :] = tokens[...]
+    bias[c] = key_bias[...]
+    wo[pl.ds(place * shard, shard), :] = w_out[...]
+
+    pl.semaphore_wait(
+        barrier,
+        4 + has_up.astype(jnp.int32) + has_down.astype(jnp.int32)
+        + cross_up.astype(jnp.int32) + cross_down.astype(jnp.int32),
+    )
+
+    def remote(source, target, send, recv, device):
+        return pltpu.make_async_remote_copy(
+            src_ref=source, dst_ref=target, send_sem=send, recv_sem=recv,
+            device_id=device, device_id_type=MESH,
+        )
+
+    def q_at(slot):
+        return wq.at[pl.ds(slot * shard, shard), :]
+
+    def o_at(slot):
+        return wo.at[pl.ds(slot * shard, shard), pl.ds(c * half, half)]
+
+    def o_other(slot):
+        return wo.at[pl.ds(slot * shard, shard), pl.ds((1 - c) * half, half)]
+
+    class Gather:
+        def __init__(self, at, send, recv, relay):
+            self.at, self.send, self.recv, self.relay = at, send, recv, relay
+
+        def copy(self, slot, k, way, device):
+            return remote(self.at(slot), self.at(slot), self.send.at[k, way], self.recv.at[slot], device)
+
+        def hop(self, slot, k):
+            return remote(self.at(slot), self.at(slot), r_send.at[k], r_recv.at[slot], sibling)
+
+        def own(self, act):
+            act(self.copy(place, 0, 0, x_peer))
+
+            @pl.when(has_up)
+            def _():
+                act(self.copy(place, 0, 1, z_up))
+
+            @pl.when(has_down)
+            def _():
+                act(self.copy(place, 0, 2, z_down))
+
+        def step(self, t, receive):
+            act = (lambda d: d.start()) if receive else (lambda d: d.wait_send())
+            for sign, reach, onward, device, way, k in (
+                (-1, z >= t, has_up, z_up, 1, t),
+                (1, z + t <= nz - 1, has_down, z_down, 2, nz - 1 + t),
+            ):
+                slot = (z + sign * t) * nx + x
+
+                @pl.when(reach)
+                def _(slot=slot, k=k):
+                    if receive:
+                        self.copy(slot, k, 0, x_peer).wait_recv()
+                    act(self.copy(slot, k, 0, x_peer))
+
+                @pl.when(jnp.logical_and(reach, onward))
+                def _(slot=slot, k=k, way=way, device=device):
+                    act(self.copy(slot, k, way, device))
+
+                if self.relay:
+                    @pl.when(reach)
+                    def _(slot=slot, k=k):
+                        act(self.hop(slot, k))
+
+        def across(self):
+            for zz in range(nz):
+                slot = zz * nx + (1 - x)
+                self.copy(slot, 0, 0, x_peer).wait_recv()
+                if self.relay:
+                    self.hop(slot, 2 * nz - 1 + zz).start()
+
+        def finish(self):
+            self.own(lambda d: d.wait_send())
+            for t in range(1, nz):
+                self.step(t, False)
+            if self.relay:
+                for zz in range(nz):
+                    slot = zz * nx + (1 - x)
+                    self.hop(slot, 2 * nz - 1 + zz).wait_send()
+
+    gather_q = Gather(q_at, q_send, q_recv, False)
+    gather_o = Gather(o_at, o_send, o_recv, True)
+    start = lambda d: d.start()
+
+    gather_q.own(start)
+
+    def tok_at(yy, cc):
+        return tok.at[yy, pl.ds(cc * rows, rows), :]
+
+    tok_copies = [
+        remote(tok_at(y, c), tok_at(y, c), t_send.at[0], t_recv.at[0], y_peer),
+        remote(tok_at(y, c), tok_at(y, c), t_send.at[1], t_recv.at[1], sibling),
+        remote(tok_at(1 - y, c), tok_at(1 - y, c), t_send.at[2], t_recv.at[2], sibling),
+        remote(bias.at[c], bias.at[c], t_send.at[3], t_recv.at[3], sibling),
+    ]
+    for k in (0, 1, 3):
+        tok_copies[k].start()
+
+    gain_a = gain_attn[...]
+
+    def norm_block(yy, cc):
+        normed[yy, pl.ds(cc * rows, rows), :] = norm_rows(tok[yy, pl.ds(cc * rows, rows), :], gain_a)
+
+    norm_block(y, c)
+    pair_row = lax.broadcasted_iota(jnp.int32, (width, 2 * head), 0)
+    pair_col = lax.broadcasted_iota(jnp.int32, (width, 2 * head), 1)
+    same = lax.rem(lax.div(pair_row, head), 2) == lax.div(pair_col, head)
+    for b in range(2):
+        wide = jnp.concatenate([w_conv[b], w_conv[b]], axis=1).astype(F32)
+        mixer[b] = jnp.where(same, wide, 0.0).astype(BF)
+
+    gather_q.step(1, True)
+    tok_copies[1].wait_recv()
+    norm_block(y, 1 - c)
+    tok_copies[0].wait_recv()
+    tok_copies[2].start()
+    gather_q.step(2, True)
+    norm_block(1 - y, c)
+    gather_o.own(start)
+    tok_copies[2].wait_recv()
+    norm_block(1 - y, 1 - c)
+    gather_q.step(3, True)
+    tok_copies[3].wait_recv()
+    bias_f[...] = jnp.concatenate([bias[0], bias[1]], axis=1).astype(F32)
+    gather_q.across()
+    gather_o.step(1, True)
+
+    def att_copy(r, to_c, k, device):
+        return remote(
+            att_out.at[r, pl.ds(to_c * rows, rows), :], att_in.at[quad],
+            a_send.at[k], a_recv.at[quad], device,
+        )
+
+    att_copies = [
+        att_copy(0, c, 0, y_peer), att_copy(0, 1 - c, 1, diagonal), att_copy(1, 1 - c, 2, sibling)
+    ]
+
+    def attend(sample, r, between):
+        projected = jnp.dot(normed[sample], wq[...], preferred_element_type=F32).astype(BF)
+        between()
+        pieces = []
+        for h in range(3):
+            queries = projected[:, h * head : (h + 1) * head] * jnp.asarray(head ** -0.5, BF)
+            keys = projected[:, part + h * head : part + (h + 1) * head]
+            vals = projected[:, 2 * part + h * head : 2 * part + (h + 1) * head]
+            scores = lax.dot_general(
+                queries, keys, (((1,), (1,)), ((), ())), preferred_element_type=F32
+            ) + bias_f[pl.ds(quad * 3 + h, 1), :]
+            expd = jnp.exp(scores - jnp.max(scores, axis=-1, keepdims=True))
+            totals = jnp.sum(expd, axis=-1, keepdims=True)
+            pieces.append(jnp.dot(expd.astype(BF), vals, preferred_element_type=F32) / totals)
+        att_out[r] = jnp.concatenate(pieces, axis=1).astype(BF)
+
+    attend(1 - y, 0, lambda: gather_o.step(2, True))
+    att_copies[0].start()
+    att_copies[1].start()
+    gather_o.step(3, True)
+    attend(y, 1, gather_o.across)
+    att_copies[2].start()
+    att_in[quad] = att_out[1, pl.ds(c * rows, rows), :]
+
+    for t in range(1, nz):
+        for sign, reach in ((-1, z >= t), (1, z + t <= nz - 1)):
+            @pl.when(reach)
+            def _(slot=(z + sign * t) * nx + x):
+                remote(o_other(slot), o_other(slot), r_send.at[0], r_recv.at[slot], sibling).wait_recv()
+    for zz in range(nz):
+        slot = zz * nx + (1 - x)
+        remote(o_other(slot), o_other(slot), r_send.at[0], r_recv.at[slot], sibling).wait_recv()
+    for source in (y * 2 + (1 - c), (1 - y) * 2 + c, (1 - y) * 2 + (1 - c)):
+        remote(att_in.at[source], att_in.at[source], a_send.at[0], a_recv.at[source], sibling).wait_recv()
+    branch = tokens[...].astype(F32)
+    for p in range(4):
+        branch = branch + jnp.dot(
+            att_in[p], wo[p * part : (p + 1) * part, :], preferred_element_type=F32
+        )
+    mid = branch.astype(BF)
+    middle[...] = mid
+    conv_in = norm_rows(mid, gain_conv[...])
+    halo[1] = conv_in
+
+    inner_up, inner_down = place < lat_count - 1, place > 0
+    to_up = remote(halo.at[1], halo.at[0], h_send.at[0], h_recv.at[0], band_up)
+    to_down = remote(halo.at[1], halo.at[2], h_send.at[1], h_recv.at[1], band_down)
+    to_side = remote(halo.at[1], other_in, h_send.at[2], h_recv.at[2], sibling)
+
+    @pl.when(inner_up)
+    def _():
+        to_up.start()
+
+    @pl.when(inner_down)
+    def _():
+        to_down.start()
+
+    to_side.start()
+
+    @pl.when(jnp.logical_not(inner_down))
+    def _():
+        halo[0] = jnp.zeros((rows, width), BF)
+
+    @pl.when(jnp.logical_not(inner_up))
+    def _():
+        halo[2] = jnp.zeros((rows, width), BF)
+
+    base = quad_off[0]
+    reach_lat = lat_half[0]
+    wide_ok = reach_lat >= 1
+    taps = [
+        [
+            lat_taps[base + r, b] if r == 1 else jnp.where(wide_ok, lat_taps[base + r, b], 0.0)
+            for b in range(2)
+        ]
+        for r in range(3)
+    ]
+    span = (lon_half[0] + 1).astype(F32)
+    limit = lon_half[0].astype(F32)
+    diff = lax.broadcasted_iota(jnp.int32, (rows, rows), 1) - lax.broadcasted_iota(
+        jnp.int32, (rows, rows), 0
+    )
+
+    def coeffs(offset):
+        offset = offset.astype(F32)
+        distance = jnp.abs(offset)
+        tent = jnp.where(distance <= limit, (1.0 - distance / span) / span, 0.0)
+        odd = tent * offset / span
+        return jnp.concatenate([tent.astype(BF), odd.astype(BF)], axis=1)
+
+    own_coeffs = coeffs(diff)
+    side_coeffs = coeffs(jnp.where(diff >= 0, diff - rows, diff + rows))
+
+    def mix(values, b):
+        return jnp.concatenate(
+            [
+                jnp.dot(
+                    values[:, p * 2 * head : (p + 1) * 2 * head],
+                    mixer[b, p * 2 * head : (p + 1) * 2 * head, :],
+                    preferred_element_type=F32,
+                )
+                for p in range(width // (2 * head))
+            ],
+            axis=1,
+        ).astype(BF)
+
+    to_side.wait_recv()
+    side_rows = other_in[...].astype(F32)
+    polar = []
+    for b in range(2):
+        gain = jnp.where(place == 0, taps[0][b], 0.0) + jnp.where(
+            place == lat_count - 1, taps[2][b], 0.0
+        )
+        polar.append(mix((gain * side_rows).astype(BF), b))
+
+    @pl.when(inner_down)
+    def _():
+        to_up.wait_recv()
+
+    @pl.when(inner_up)
+    def _():
+        to_down.wait_recv()
+
+    for b in range(2):
+        summed = (
+            taps[0][b] * halo[0].astype(F32)
+            + taps[1][b] * halo[1].astype(F32)
+            + taps[2][b] * halo[2].astype(F32)
+        ).astype(BF)
+        blended = (mix(summed, b).astype(F32) + polar[b].astype(F32)).astype(BF)
+        mixed_all[c, b * rows : (b + 1) * rows, :] = blended
+    to_mix = remote(mixed_all.at[c], mixed_all.at[c], h_send.at[3], h_recv.at[3], sibling)
+    to_mix.start()
+    total = middle[...].astype(F32) + jnp.dot(own_coeffs, mixed_all[c], preferred_element_type=F32)
+    to_mix.wait_recv()
+    total = total + jnp.dot(side_coeffs, mixed_all[1 - c], preferred_element_type=F32)
+    out[...] = total.astype(BF)
+
+    gather_q.finish()
+    gather_o.finish()
+    for d in tok_copies + att_copies + [to_side, to_mix]:
+        d.wait_send()
+
+    @pl.when(inner_up)
+    def _():
+        to_up.wait_send()
+
+    @pl.when(inner_down)
+    def _():
+        to_down.wait_send()
+
+
+def fused_device(
+    tokens, gain_attn, w_qkv, key_bias, w_out, gain_conv, w_conv, lat_taps, lon_half, lat_half, quad_off
+):
+    rows, width = tokens.shape[1:]
+    shard = w_qkv.shape[0]
+    heads = key_bias.shape[1]
+    lat_count = width // shard
+    nx = 2
+    nz = lat_count // nx
+    vmem = pl.BlockSpec(memory_space=pltpu.VMEM)
+    smem = pl.BlockSpec(memory_space=pltpu.SMEM)
+    dma = pltpu.SemaphoreType.DMA
+    kinds = 2 * nz - 1
+    out = pl.pallas_call(
+        lambda *refs: fused_kernel(nx, nz, *refs),
+        out_shape=jax.ShapeDtypeStruct((rows, width), BF),
+        in_specs=[smem] * 4 + [vmem] * 7,
+        out_specs=vmem,
+        scratch_shapes=[
+            pltpu.VMEM((width, 3 * width // 4), BF),
+            pltpu.VMEM((width, width), BF),
+            pltpu.VMEM((2, 2 * rows, width), BF),
+            pltpu.VMEM((2, 2 * rows, width), BF),
+            pltpu.VMEM((2, heads, rows), BF),
+            pltpu.VMEM((heads, 2 * rows), F32),
+            pltpu.VMEM((2, 2 * rows, width // 4), BF),
+            pltpu.VMEM((4, rows, width // 4), BF),
+            pltpu.VMEM((3, rows, width), BF),
+            pltpu.VMEM((rows, width), BF),
+            pltpu.VMEM((2, width, 128), BF),
+            pltpu.VMEM((2, 2 * rows, width), BF),
+            pltpu.VMEM((rows, width), BF),
+            dma((kinds, 3)),
+            dma((lat_count,)),
+            dma((kinds, 3)),
+            dma((lat_count,)),
+            dma((kinds + nz,)),
+            dma((lat_count,)),
+            dma((4,)),
+            dma((4,)),
+            dma((3,)),
+            dma((4,)),
+            dma((4,)),
+            dma((4,)),
+        ],
+        compiler_params=pltpu.CompilerParams(
+            collective_id=0, has_side_effects=True, vmem_limit_bytes=48 * 1024 * 1024
+        ),
+    )(
+        lat_taps, lon_half, lat_half, quad_off,
+        tokens[0], gain_attn[None], w_qkv, key_bias[0], w_out, gain_conv[None], w_conv,
+    )
+    return out[None]
+
+
 def solution(mesh):
+    sizes = (mesh.shape["groups"], mesh.shape["lat"], mesh.shape["lon"])
     return jax.shard_map(
-        per_device,
+        fused_device if sizes == (2, 8, 2) else per_device,
         mesh=mesh,
         in_specs=(
             P(("groups", "lat"), "lon", None),

time: 146 us -> 47.8 us (0.33)
  the two profiles are of different devices: /device:TPU:9 before, /device:TPU:0 now
where the time goes in v1:
time: 47.8 us; the launch traced here: 47.5 us
  Pallas kernels  40.5 us (85%)
  local copies, waits for them, and re-layouts  4.93 us (10%)
  between operations  2.05 us (4%)
    pallas_call x1, Pallas kernels, fused_device(): pl.pallas_call(lambda *refs: fused_kernel(nx, nz, *refs), out_shape=jax.S...  40.5 us
    unnamed x11, local copies, waits for them, and re-layouts  3.55 us

profile of v1, /device:TPU:0, one launch (start us, length us, event | category | flops | bytes accessed | tf_op | source)
XLA Modules:
  0.0 47.5 jit_solution(6117194071097761334)
XLA Ops:
  0.0 0.0 copy-start
  2.0 0.7 %broadcast_in_dim.9.refs_5_ = f32[1,768]{1,0:T(1,128)S(1)} reshape(f32[768]{0:T(1024)} %param.12) | data formatting | bytes 6144 | tf_op jit(solution)/shard_map/broadcast_in_dim | solution.py:605
  2.7 0.7 %broadcast_in_dim.10.refs_9_ = f32[1,768]{1,0:T(1,128)S(1)} reshape(f32[768]{0:T(1024)} %param.16) | data formatting | bytes 6144 | tf_op jit(solution)/shard_map/broadcast_in_dim | solution.py:605
  3.4 0.8 %copy.12.refs_0_ = f32[16,2]{1,0:T(8,128)S(1)} copy(f32[16,2]{0,1:T(2,128)} %param.18) | data formatting | bytes 256 | tf_op args[7]
  4.1 0.0 copy-start.2
  4.1 0.0 copy-start.3
  4.1 1.2 %copy.13.refs_10_ = bf16[2,768,64]{2,1,0:T(8,128)(2,1)S(1)} copy(bf16[2,768,64]{1,2,0:T(8,128)(2,1)} %param.17) | data formatting | bytes 393216 | tf_op args[6]
  5.3 0.0 copy-done
  5.3 0.0 copy-done.2
  5.3 0.0 copy-done.3
  5.4 0.0 copy-start.1
  5.4 0.9 %copy-done.1 = bf16[1,128,768]{2,1,0:T(8,128)(2,1)S(1)} copy-done((bf16[1,128,768]{2,1,0:T(8,128)(2,1)S(1)}, bf16[1,128,768]{2,1,0:T(8,128)(2,1)}, u32[]{:S(2)}) %copy-start.1) | copy-done | bytes 196632
  6.3 40.5 %shard_map.109 = bf16[128,768]{1,0:T(8,128)(2,1)S(1)} custom-call(f32[16,2]{1,0:T(8,128)S(1)} %copy.12.refs_0_, s32[1]{0:T(128)S(6)} %copy.15.refs_1_, s32[1]{0:T(128)S(6)} %copy.16.refs_2_, s32[1]{0:T(128)S(6)} %copy.17.refs_3_, bf16[128,768]{1,0:T(8,128)(2,1)S(1)} %bitcast.4, f32[1,768]{1,0:T(1,128)S(1)} %broadcast_in_dim.9.refs_5_, ...), custom_call_target="tpu_custom_call" | custom-call | tf_op jit(solution)/shard_map/pallas_call | solution.py:568
  46.8 0.7 %copy.18 = bf16[1,128,768]{2,1,0:T(8,128)(2,1)} copy(bf16[1,128,768]{2,1,0:T(8,128)(2,1)S(1)} %bitcast.3) | data formatting | bytes 393216
Async XLA Ops:
  0.0 5.3 %copy-start = (bf16[96,2304]{1,0:T(8,128)(2,1)S(1)}, bf16[96,2304]{1,0:T(8,128)(2,1)}, u32[]{:S(2)}) copy-start(bf16[96,2304]{1,0:T(8,128)(2,1)} %refs_6_.1) | copy-start | bytes 1327108
  4.1 1.2 %copy-start.2 = (bf16[96,768]{1,0:T(8,128)(2,1)S(1)}, bf16[96,768]{1,0:T(8,128)(2,1)}, u32[]{:S(2)}) copy-start(bf16[96,768]{1,0:T(8,128)(2,1)} %refs_8_.1) | copy-start | bytes 442372
  4.1 1.2 %copy-start.3 = (bf16[1,12,128]{2,1,0:T(8,128)(2,1)S(1)}, bf16[1,12,128]{2,1,0:T(8,128)(2,1)}, u32[]{:S(2)}) copy-start(bf16[1,12,128]{2,1,0:T(8,128)(2,1)} %param.14) | copy-start | bytes 9220
  5.4 0.9 %copy-start.1 = (bf16[1,128,768]{2,1,0:T(8,128)(2,1)S(1)}, bf16[1,128,768]{2,1,0:T(8,128)(2,1)}, u32[]{:S(2)}) copy-start(bf16[1,128,768]{2,1,0:T(8,128)(2,1)} %param.11) | copy-start | bytes 589828

commit v2 on v1

--- a/solution.py
+++ b/solution.py
@@ -211,11 +211,12 @@
 
 def fused_kernel(
     nx, nz,
-    lat_taps, lon_half, lat_half, quad_off,
-    tokens, gain_attn, w_qkv, key_bias, w_out, gain_conv, w_conv,
+    lat_taps_h, lon_half_h, lat_half_h, quad_off_h,
+    tokens_h, gain_attn_h, w_qkv_h, key_bias_h, w_out_h, gain_conv_h, w_conv_h,
     out,
+    lat_taps, lon_half, lat_half, quad_off, gain_attn, w_qkv, gain_conv, w_conv, load,
     wq, wo, tok, normed, bias, bias_f, att_out, att_in, halo, other_in, mixer, mixed_all, middle,
-    q_send, q_recv, o_send, o_recv, r_send, r_recv, t_send, t_recv, a_send, a_recv, h_send, h_recv,
+    q_send, q_recv, o_send, o_recv, r_send, r_recv, t_send, t_recv, a_send, a_recv, h_send, h_recv, n_send, n_recv, f_send, f_recv,
 ):
     y, place, c = lax.axis_index("groups"), lax.axis_index("lat"), lax.axis_index("lon")
     z, x = lax.div(place, nx), lax.rem(place, nx)
@@ -225,14 +226,11 @@
     sibling = (y, place, 1 - c)
     y_peer = (1 - y, place, c)
     diagonal = (1 - y, place, 1 - c)
-    band_up, band_down = (y, place + 1, c), (y, place - 1, c)
     has_up, has_down = z < nz - 1, z > 0
-    cross_up = jnp.logical_and(x == 1, has_up)
-    cross_down = jnp.logical_and(x == 0, has_down)
     lat_count = nx * nz
     shard = w_qkv.shape[0]
-    width = tokens.shape[1]
-    rows = tokens.shape[0]
+    width = tokens_h.shape[1]
+    rows = tokens_h.shape[0]
     head = 64
     part = width // 4
     half = width // 2
@@ -244,12 +242,33 @@
 
     for device in (x_peer, sibling, y_peer, diagonal):
         greet(device)
-    for cond, device in (
-        (has_up, z_up), (has_down, z_down), (cross_up, band_up), (cross_down, band_down)
-    ):
+    for cond, device in ((has_up, z_up), (has_down, z_down)):
         @pl.when(cond)
         def _(device=device):
             greet(device)
+
+    own_tokens = tok.at[y, pl.ds(c * rows, rows), :]
+    loads = [
+        pltpu.make_async_copy(source, target, load.at[k])
+        for k, (source, target) in enumerate(
+            (
+                (w_qkv_h, w_qkv),
+                (tokens_h, own_tokens),
+                (gain_attn_h, gain_attn),
+                (w_conv_h, w_conv),
+                (key_bias_h, bias.at[c]),
+                (w_out_h, wo.at[pl.ds(place * shard, shard), :]),
+                (gain_conv_h, gain_conv),
+                (lat_taps_h, lat_taps),
+                (lon_half_h, lon_half),
+                (lat_half_h, lat_half),
+                (quad_off_h, quad_off),
+            )
+        )
+    ]
+    for copy in loads:
+        copy.start()
+    loads[0].wait()
 
     for pick in range(4):
         @pl.when(quad == pick)
@@ -258,14 +277,11 @@
                 [w_qkv[:, j * width + pick * part : j * width + (pick + 1) * part] for j in range(3)],
                 axis=1,
             )
-    tok[y, pl.ds(c * rows, rows), :] = tokens[...]
-    bias[c] = key_bias[...]
-    wo[pl.ds(place * shard, shard), :] = w_out[...]
+    loads[1].wait()
 
     pl.semaphore_wait(
         barrier,
-        4 + has_up.astype(jnp.int32) + has_down.astype(jnp.int32)
-        + cross_up.astype(jnp.int32) + cross_down.astype(jnp.int32),
+        4 + has_up.astype(jnp.int32) + has_down.astype(jnp.int32),
     )
 
     def remote(source, target, send, recv, device):
@@ -274,63 +290,70 @@
             device_id=device, device_id_type=MESH,
         )
 
-    def q_at(slot):
-        return wq.at[pl.ds(slot * shard, shard), :]
-
-    def o_at(slot):
+    def q_at(slot, h):
+        return wq.at[pl.ds(slot * shard + h * (shard // 2), shard // 2), :]
+
+    def o_at(slot, h=0):
         return wo.at[pl.ds(slot * shard, shard), pl.ds(c * half, half)]
 
     def o_other(slot):
         return wo.at[pl.ds(slot * shard, shard), pl.ds((1 - c) * half, half)]
 
     class Gather:
-        def __init__(self, at, send, recv, relay):
+        def __init__(self, at, send, recv, relay, chunks):
             self.at, self.send, self.recv, self.relay = at, send, recv, relay
-
-        def copy(self, slot, k, way, device):
-            return remote(self.at(slot), self.at(slot), self.send.at[k, way], self.recv.at[slot], device)
+            self.chunks = range(chunks)
+
+        def copy(self, slot, k, way, device, h):
+            return remote(
+                self.at(slot, h), self.at(slot, h),
+                self.send.at[k, way, h], self.recv.at[slot, h], device,
+            )
 
         def hop(self, slot, k):
             return remote(self.at(slot), self.at(slot), r_send.at[k], r_recv.at[slot], sibling)
 
         def own(self, act):
-            act(self.copy(place, 0, 0, x_peer))
-
-            @pl.when(has_up)
-            def _():
-                act(self.copy(place, 0, 1, z_up))
-
-            @pl.when(has_down)
-            def _():
-                act(self.copy(place, 0, 2, z_down))
+            for h in self.chunks:
+                @pl.when(has_up)
+                def _(h=h):
+                    act(self.copy(place, 0, 1, z_up, h))
+
+                @pl.when(has_down)
+                def _(h=h):
+                    act(self.copy(place, 0, 2, z_down, h))
+
+                act(self.copy(place, 0, 0, x_peer, h))
 
         def step(self, t, receive):
             act = (lambda d: d.start()) if receive else (lambda d: d.wait_send())
-            for sign, reach, onward, device, way, k in (
-                (-1, z >= t, has_up, z_up, 1, t),
-                (1, z + t <= nz - 1, has_down, z_down, 2, nz - 1 + t),
-            ):
-                slot = (z + sign * t) * nx + x
-
-                @pl.when(reach)
-                def _(slot=slot, k=k):
-                    if receive:
-                        self.copy(slot, k, 0, x_peer).wait_recv()
-                    act(self.copy(slot, k, 0, x_peer))
-
-                @pl.when(jnp.logical_and(reach, onward))
-                def _(slot=slot, k=k, way=way, device=device):
-                    act(self.copy(slot, k, way, device))
-
-                if self.relay:
+            for h in self.chunks:
+                for sign, reach, onward, device, way, k in (
+                    (-1, z >= t, has_up, z_up, 1, t),
+                    (1, z + t <= nz - 1, has_down, z_down, 2, nz - 1 + t),
+                ):
+                    slot = (z + sign * t) * nx + x
+
                     @pl.when(reach)
-                    def _(slot=slot, k=k):
-                        act(self.hop(slot, k))
+                    def _(slot=slot, k=k, h=h):
+                        if receive:
+                            self.copy(slot, k, 0, x_peer, h).wait_recv()
+
+                    @pl.when(jnp.logical_and(reach, onward))
+                    def _(slot=slot, k=k, way=way, device=device, h=h):
+                        act(self.copy(slot, k, way, device, h))
+
+                    @pl.when(reach)
+                    def _(slot=slot, k=k, h=h):
+                        act(self.copy(slot, k, 0, x_peer, h))
+                        if self.relay:
+                            act(self.hop(slot, k))
 
         def across(self):
             for zz in range(nz):
                 slot = zz * nx + (1 - x)
-                self.copy(slot, 0, 0, x_peer).wait_recv()
+                for h in self.chunks:
+                    self.copy(slot, 0, 0, x_peer, h).wait_recv()
                 if self.relay:
                     self.hop(slot, 2 * nz - 1 + zz).start()
 
@@ -343,8 +366,8 @@
                     slot = zz * nx + (1 - x)
                     self.hop(slot, 2 * nz - 1 + zz).wait_send()
 
-    gather_q = Gather(q_at, q_send, q_recv, False)
-    gather_o = Gather(o_at, o_send, o_recv, True)
+    gather_q = Gather(q_at, q_send, q_recv, False, 2)
+    gather_o = Gather(o_at, o_send, o_recv, True, 1)
     start = lambda d: d.start()
 
     gather_q.own(start)
@@ -358,20 +381,23 @@
         remote(tok_at(1 - y, c), tok_at(1 - y, c), t_send.at[2], t_recv.at[2], sibling),
         remote(bias.at[c], bias.at[c], t_send.at[3], t_recv.at[3], sibling),
     ]
-    for k in (0, 1, 3):
-        tok_copies[k].start()
-
-    gain_a = gain_attn[...]
+    tok_copies[0].start()
+    tok_copies[1].start()
+    loads[4].wait()
+    tok_copies[3].start()
+    loads[2].wait()
+    gain_a = gain_attn[...][None]
 
     def norm_block(yy, cc):
         normed[yy, pl.ds(cc * rows, rows), :] = norm_rows(tok[yy, pl.ds(cc * rows, rows), :], gain_a)
 
     norm_block(y, c)
-    pair_row = lax.broadcasted_iota(jnp.int32, (width, 2 * head), 0)
-    pair_col = lax.broadcasted_iota(jnp.int32, (width, 2 * head), 1)
-    same = lax.rem(lax.div(pair_row, head), 2) == lax.div(pair_col, head)
+    loads[3].wait()
+    pair_row = lax.broadcasted_iota(jnp.int32, (2 * head, width), 0)
+    pair_col = lax.broadcasted_iota(jnp.int32, (2 * head, width), 1)
+    same = lax.rem(lax.div(pair_col, head), 2) == lax.div(pair_row, head)
     for b in range(2):
-        wide = jnp.concatenate([w_conv[b], w_conv[b]], axis=1).astype(F32)
+        wide = jnp.concatenate([w_conv[b], w_conv[b]], axis=0).astype(F32)
         mixer[b] = jnp.where(same, wide, 0.0).astype(BF)
 
     gather_q.step(1, True)
@@ -381,6 +407,7 @@
     tok_copies[2].start()
     gather_q.step(2, True)
     norm_block(1 - y, c)
+    loads[5].wait()
     gather_o.own(start)
     tok_copies[2].wait_recv()
     norm_block(1 - y, 1 - c)
@@ -434,45 +461,55 @@
         remote(o_other(slot), o_other(slot), r_send.at[0], r_recv.at[slot], sibling).wait_recv()
     for source in (y * 2 + (1 - c), (1 - y) * 2 + c, (1 - y) * 2 + (1 - c)):
         remote(att_in.at[source], att_in.at[source], a_send.at[0], a_recv.at[source], sibling).wait_recv()
-    branch = tokens[...].astype(F32)
+    branch = tok[y, pl.ds(c * rows, rows), :].astype(F32)
     for p in range(4):
         branch = branch + jnp.dot(
             att_in[p], wo[p * part : (p + 1) * part, :], preferred_element_type=F32
         )
     mid = branch.astype(BF)
     middle[...] = mid
-    conv_in = norm_rows(mid, gain_conv[...])
+    for k in range(6, 11):
+        loads[k].wait()
+    conv_in = norm_rows(mid, gain_conv[...][None])
     halo[1] = conv_in
 
-    inner_up, inner_down = place < lat_count - 1, place > 0
-    to_up = remote(halo.at[1], halo.at[0], h_send.at[0], h_recv.at[0], band_up)
-    to_down = remote(halo.at[1], halo.at[2], h_send.at[1], h_recv.at[1], band_down)
+    near, far = 2 * (1 - x), 2 * x
+    passes = jnp.logical_or(jnp.logical_and(x == 0, has_up), jnp.logical_and(x == 1, has_down))
+    gets = jnp.logical_or(jnp.logical_and(x == 0, has_down), jnp.logical_and(x == 1, has_up))
+    onward = (y, place + nx * (1 - 2 * x), c)
+    pieces = 4
+    piece = rows // pieces
+
+    def halo_at(which, k):
+        return halo.at[which, pl.ds(k * piece, piece), :]
+
+    to_near = [
+        remote(halo_at(1, k), halo_at(far, k), n_send.at[k], n_recv.at[k], x_peer)
+        for k in range(pieces)
+    ]
+    from_near = [
+        remote(halo_at(1, k), halo_at(near, k), n_send.at[k], n_recv.at[k], x_peer)
+        for k in range(pieces)
+    ]
+    to_far = [
+        remote(halo_at(near, k), halo_at(far, k), f_send.at[k], f_recv.at[k], onward)
+        for k in range(pieces)
+    ]
+    for d in to_near:
+        d.start()
     to_side = remote(halo.at[1], other_in, h_send.at[2], h_recv.at[2], sibling)
-
-    @pl.when(inner_up)
+    to_side.start()
+
+    @pl.when(jnp.logical_not(gets))
     def _():
-        to_up.start()
-
-    @pl.when(inner_down)
-    def _():
-        to_down.start()
-
-    to_side.start()
-
-    @pl.when(jnp.logical_not(inner_down))
-    def _():
-        halo[0] = jnp.zeros((rows, width), BF)
-
-    @pl.when(jnp.logical_not(inner_up))
-    def _():
-        halo[2] = jnp.zeros((rows, width), BF)
+        halo[far] = jnp.zeros((rows, width), BF)
 
     base = quad_off[0]
     reach_lat = lat_half[0]
     wide_ok = reach_lat >= 1
     taps = [
         [
-            lat_taps[base + r, b] if r == 1 else jnp.where(wide_ok, lat_taps[base + r, b], 0.0)
+            lat_taps[b, base + r] if r == 1 else jnp.where(wide_ok, lat_taps[b, base + r], 0.0)
             for b in range(2)
         ]
         for r in range(3)
@@ -496,9 +533,10 @@
     def mix(values, b):
         return jnp.concatenate(
             [
-                jnp.dot(
+                lax.dot_general(
                     values[:, p * 2 * head : (p + 1) * 2 * head],
-                    mixer[b, p * 2 * head : (p + 1) * 2 * head, :],
+                    mixer[b, :, p * 2 * head : (p + 1) * 2 * head],
+                    (((1,), (1,)), ((), ())),
                     preferred_element_type=F32,
                 )
                 for p in range(width // (2 * head))
@@ -506,6 +544,13 @@
             axis=1,
         ).astype(BF)
 
+    for k in range(pieces):
+        from_near[k].wait_recv()
+
+        @pl.when(passes)
+        def _(k=k):
+            to_far[k].start()
+
     to_side.wait_recv()
     side_rows = other_in[...].astype(F32)
     polar = []
@@ -515,13 +560,10 @@
         )
         polar.append(mix((gain * side_rows).astype(BF), b))
 
-    @pl.when(inner_down)
+    @pl.when(gets)
     def _():
-        to_up.wait_recv()
-
-    @pl.when(inner_up)
-    def _():
-        to_down.wait_recv()
+        for d in to_far:
+            d.wait_recv()
 
     for b in range(2):
         summed = (
@@ -543,13 +585,13 @@
     for d in tok_copies + att_copies + [to_side, to_mix]:
         d.wait_send()
 
-    @pl.when(inner_up)
+    for d in to_near:
+        d.wait_send()
+
+    @pl.when(passes)
     def _():
-        to_up.wait_send()
-
-    @pl.when(inner_down)
-    def _():
-        to_down.wait_send()
+        for d in to_far:
+            d.wait_send()
 
 
 def fused_device(
@@ -562,15 +604,24 @@
     nx = 2
     nz = lat_count // nx
     vmem = pl.BlockSpec(memory_space=pltpu.VMEM)
-    smem = pl.BlockSpec(memory_space=pltpu.SMEM)
+    anywhere = pl.BlockSpec(memory_space=pltpu.HBM)
     dma = pltpu.SemaphoreType.DMA
     kinds = 2 * nz - 1
     out = pl.pallas_call(
         lambda *refs: fused_kernel(nx, nz, *refs),
         out_shape=jax.ShapeDtypeStruct((rows, width), BF),
-        in_specs=[smem] * 4 + [vmem] * 7,
+        in_specs=[anywhere] * 11,
         out_specs=vmem,
         scratch_shapes=[
+            pltpu.SMEM((2, lat_taps.shape[0]), F32),
+            pltpu.SMEM((1,), jnp.int32),
+            pltpu.SMEM((1,), jnp.int32),
+            pltpu.SMEM((1,), jnp.int32),
+            pltpu.VMEM((width,), F32),
+            pltpu.VMEM(w_qkv.shape, BF),
+            pltpu.VMEM((width,), F32),
+            pltpu.VMEM((2, 64, width), BF),
+            dma((11,)),
             pltpu.VMEM((width, 3 * width // 4), BF),
             pltpu.VMEM((width, width), BF),
             pltpu.VMEM((2, 2 * rows, width), BF),
@@ -581,13 +632,13 @@
             pltpu.VMEM((4, rows, width // 4), BF),
             pltpu.VMEM((3, rows, width), BF),
             pltpu.VMEM((rows, width), BF),
-            pltpu.VMEM((2, width, 128), BF),
+            pltpu.VMEM((2, 128, width), BF),
             pltpu.VMEM((2, 2 * rows, width), BF),
             pltpu.VMEM((rows, width), BF),
-            dma((kinds, 3)),
-            dma((lat_count,)),
-            dma((kinds, 3)),
-            dma((lat_count,)),
+            dma((kinds, 3, 2)),
+            dma((lat_count, 2)),
+            dma((kinds, 3, 1)),
+            dma((lat_count, 1)),
             dma((kinds + nz,)),
             dma((lat_count,)),
             dma((4,)),
@@ -596,13 +647,17 @@
             dma((4,)),
             dma((4,)),
             dma((4,)),
+            dma((4,)),
+            dma((4,)),
+            dma((4,)),
+            dma((4,)),
         ],
         compiler_params=pltpu.CompilerParams(
-            collective_id=0, has_side_effects=True, vmem_limit_bytes=48 * 1024 * 1024
+            collective_id=0, has_side_effects=True, vmem_limit_bytes=63 * 1024 * 1024
         ),
     )(
-        lat_taps, lon_half, lat_half, quad_off,
-        tokens[0], gain_attn[None], w_qkv, key_bias[0], w_out, gain_conv[None], w_conv,
+        lat_taps.T, lon_half, lat_half, quad_off,
+        tokens[0], gain_attn, w_qkv, key_bias[0], w_out, gain_conv, jnp.swapaxes(w_conv, 1, 2),
     )
     return out[None]
 

time: 47.8 us -> 46.1 us (0.964)
  the two profiles are of different devices: /device:TPU:0 before, /device:TPU:9 now
where the time goes in v2:
time: 46.1 us; the launch traced here: 45.9 us
  Pallas kernels  42.3 us (92%)
  between operations  1.95 us (4%)
  local copies, waits for them, and re-layouts  1.62 us (4%)
    pallas_call x1, Pallas kernels, fused_device(): pl.pallas_call(lambda *refs: fused_kernel(nx, nz, *refs), out_shape=jax.S...  42.3 us
    unnamed x1, local copies, waits for them, and re-layouts  1.62 us

profile of v2, /device:TPU:9, one launch (start us, length us, event | category | flops | bytes accessed | tf_op | source)
XLA Modules:
  0.0 45.9 jit_solution(3982437598455145244)
XLA Ops:
  1.9 42.3 %shard_map.109 = bf16[128,768]{1,0:T(8,128)(2,1)} custom-call(f32[2,16]{1,0:T(2,128)} %bitcast.9, s32[1]{0:T(128)S(6)} %copy.13.refs_1_, s32[1]{0:T(128)S(6)} %copy.14.refs_2_, s32[1]{0:T(128)S(6)} %copy.15.refs_3_, bf16[128,768]{1,0:T(8,128)(2,1)} %bitcast.6, f32[768]{0:T(1024)} %refs_5_.1, bf16[96,2304]{1,0:T(8,128)(2,1)} %refs_6_.1, ...), custom_call_target="tpu_custom_call" | custom-call | tf_op jit(solution)/shard_map/pallas_call | solution.py:610
  44.3 1.6 %copy.16 = bf16[1,128,768]{2,1,0:T(8,128)(2,1)} copy(bf16[1,128,768]{2,1,0:T(8,128)(2,1)} %bitcast.5) | data formatting | bytes 393216

commit v3 on v2

--- a/solution.py
+++ b/solution.py
@@ -217,6 +217,7 @@
     lat_taps, lon_half, lat_half, quad_off, gain_attn, w_qkv, gain_conv, w_conv, load,
     wq, wo, tok, normed, bias, bias_f, att_out, att_in, halo, other_in, mixer, mixed_all, middle,
     q_send, q_recv, o_send, o_recv, r_send, r_recv, t_send, t_recv, a_send, a_recv, h_send, h_recv, n_send, n_recv, f_send, f_recv,
+    y_send, y_recv, g_send, g_recv,
 ):
     y, place, c = lax.axis_index("groups"), lax.axis_index("lat"), lax.axis_index("lon")
     z, x = lax.div(place, nx), lax.rem(place, nx)
@@ -293,15 +294,14 @@
     def q_at(slot, h):
         return wq.at[pl.ds(slot * shard + h * (shard // 2), shard // 2), :]
 
-    def o_at(slot, h=0):
-        return wo.at[pl.ds(slot * shard, shard), pl.ds(c * half, half)]
-
-    def o_other(slot):
-        return wo.at[pl.ds(slot * shard, shard), pl.ds((1 - c) * half, half)]
+    def o_at(slot, yy, cc):
+        return wo.at[
+            pl.ds(slot * shard + yy * (shard // 2), shard // 2), pl.ds(cc * half, half)
+        ]
 
     class Gather:
-        def __init__(self, at, send, recv, relay, chunks):
-            self.at, self.send, self.recv, self.relay = at, send, recv, relay
+        def __init__(self, at, send, recv, chunks):
+            self.at, self.send, self.recv = at, send, recv
             self.chunks = range(chunks)
 
         def copy(self, slot, k, way, device, h):
@@ -309,9 +309,6 @@
                 self.at(slot, h), self.at(slot, h),
                 self.send.at[k, way, h], self.recv.at[slot, h], device,
             )
-
-        def hop(self, slot, k):
-            return remote(self.at(slot), self.at(slot), r_send.at[k], r_recv.at[slot], sibling)
 
         def own(self, act):
             for h in self.chunks:
@@ -346,28 +343,96 @@
                     @pl.when(reach)
                     def _(slot=slot, k=k, h=h):
                         act(self.copy(slot, k, 0, x_peer, h))
-                        if self.relay:
-                            act(self.hop(slot, k))
 
         def across(self):
             for zz in range(nz):
                 slot = zz * nx + (1 - x)
                 for h in self.chunks:
                     self.copy(slot, 0, 0, x_peer, h).wait_recv()
-                if self.relay:
-                    self.hop(slot, 2 * nz - 1 + zz).start()
 
         def finish(self):
             self.own(lambda d: d.wait_send())
             for t in range(1, nz):
                 self.step(t, False)
-            if self.relay:
-                for zz in range(nz):
-                    slot = zz * nx + (1 - x)
-                    self.hop(slot, 2 * nz - 1 + zz).wait_send()
-
-    gather_q = Gather(q_at, q_send, q_recv, False, 2)
-    gather_o = Gather(o_at, o_send, o_recv, True, 1)
+
+    others = [(None, z * nx + (1 - x), ((has_up, 1, z_up), (has_down, 2, z_down)))]
+    for t in range(1, nz):
+        for sign, reach, going, way, device in (
+            (-1, z >= t, has_up, 1, z_up), (1, z + t <= nz - 1, has_down, 2, z_down)
+        ):
+            for xx in range(nx):
+                others.append(
+                    (
+                        reach,
+                        (z + sign * t) * nx + xx,
+                        ((jnp.logical_and(reach, going), way, device),),
+                    )
+                )
+
+    def when(cond, run):
+        if cond is None:
+            run()
+        else:
+            pl.when(cond)(run)
+
+    def o_copy(slot, k, way, device):
+        return remote(
+            o_at(slot, y, c), o_at(slot, y, c), o_send.at[k, way], o_recv.at[slot], device
+        )
+
+    def o_side(slot, k):
+        return remote(o_at(slot, y, c), o_at(slot, y, c), r_send.at[k], r_recv.at[slot], sibling)
+
+    def o_cross(slot, k):
+        return remote(o_at(slot, y, c), o_at(slot, y, c), y_send.at[k], y_recv.at[slot], y_peer)
+
+    def o_last(slot, k):
+        return remote(
+            o_at(slot, 1 - y, c), o_at(slot, 1 - y, c), g_send.at[k], g_recv.at[slot], sibling
+        )
+
+    def o_own(act):
+        for cond, way, device in ((None, 0, x_peer), (has_up, 1, z_up), (has_down, 2, z_down)):
+            when(cond, lambda way=way, device=device: act(o_copy(place, 13, way, device)))
+
+    def o_forward(k, act):
+        reach, slot, targets = others[k]
+        for cond, way, device in targets:
+            when(cond, lambda way=way, device=device: act(o_copy(slot, k, way, device)))
+
+        def hand():
+            act(o_cross(slot, k))
+            act(o_side(slot, k))
+
+        when(reach, hand)
+
+    def o_step(ks):
+        for k in ks:
+            reach, slot, _ = others[k]
+            when(reach, lambda slot=slot: o_copy(slot, 0, 0, x_peer).wait_recv())
+            o_forward(k, lambda d: d.start())
+
+    def o_collect():
+        for k, (reach, slot, _) in enumerate(others):
+            def run(slot=slot, k=k):
+                o_cross(slot, k).wait_recv()
+                o_last(slot, k).start()
+
+            when(reach, run)
+        for k, (reach, slot, _) in enumerate(others):
+            def run(slot=slot, k=k):
+                o_side(slot, k).wait_recv()
+                o_last(slot, k).wait_recv()
+
+            when(reach, run)
+
+    def o_finish():
+        o_own(lambda d: d.wait_send())
+        for k, (reach, slot, _) in enumerate(others):
+            o_forward(k, lambda d: d.wait_send())
+            when(reach, lambda slot=slot, k=k: o_last(slot, k).wait_send())
+
+    gather_q = Gather(q_at, q_send, q_recv, 2)
     start = lambda d: d.start()
 
     gather_q.own(start)
@@ -408,14 +473,15 @@
     gather_q.step(2, True)
     norm_block(1 - y, c)
     loads[5].wait()
-    gather_o.own(start)
+    o_own(start)
     tok_copies[2].wait_recv()
     norm_block(1 - y, 1 - c)
     gather_q.step(3, True)
+    o_step([0])
     tok_copies[3].wait_recv()
     bias_f[...] = jnp.concatenate([bias[0], bias[1]], axis=1).astype(F32)
     gather_q.across()
-    gather_o.step(1, True)
+    o_step(range(1, 5))
 
     def att_copy(r, to_c, k, device):
         return remote(
@@ -443,22 +509,16 @@
             pieces.append(jnp.dot(expd.astype(BF), vals, preferred_element_type=F32) / totals)
         att_out[r] = jnp.concatenate(pieces, axis=1).astype(BF)
 
-    attend(1 - y, 0, lambda: gather_o.step(2, True))
+    attend(1 - y, 0, lambda: None)
     att_copies[0].start()
     att_copies[1].start()
-    gather_o.step(3, True)
-    attend(y, 1, gather_o.across)
+    o_step(range(5, 9))
+    attend(y, 1, lambda: None)
     att_copies[2].start()
+    o_step(range(9, 13))
     att_in[quad] = att_out[1, pl.ds(c * rows, rows), :]
 
-    for t in range(1, nz):
-        for sign, reach in ((-1, z >= t), (1, z + t <= nz - 1)):
-            @pl.when(reach)
-            def _(slot=(z + sign * t) * nx + x):
-                remote(o_other(slot), o_other(slot), r_send.at[0], r_recv.at[slot], sibling).wait_recv()
-    for zz in range(nz):
-        slot = zz * nx + (1 - x)
-        remote(o_other(slot), o_other(slot), r_send.at[0], r_recv.at[slot], sibling).wait_recv()
+    o_collect()
     for source in (y * 2 + (1 - c), (1 - y) * 2 + c, (1 - y) * 2 + (1 - c)):
         remote(att_in.at[source], att_in.at[source], a_send.at[0], a_recv.at[source], sibling).wait_recv()
     branch = tok[y, pl.ds(c * rows, rows), :].astype(F32)
@@ -581,7 +641,7 @@
     out[...] = total.astype(BF)
 
     gather_q.finish()
-    gather_o.finish()
+    o_finish()
     for d in tok_copies + att_copies + [to_side, to_mix]:
         d.wait_send()
 
@@ -637,10 +697,10 @@
             pltpu.VMEM((rows, width), BF),
             dma((kinds, 3, 2)),
             dma((lat_count, 2)),
-            dma((kinds, 3, 1)),
-            dma((lat_count, 1)),
-            dma((kinds + nz,)),
+            dma((14, 3)),
             dma((lat_count,)),
+            dma((13,)),
+            dma((lat_count,)),
             dma((4,)),
             dma((4,)),
             dma((3,)),
@@ -651,6 +711,10 @@
             dma((4,)),
             dma((4,)),
             dma((4,)),
+            dma((13,)),
+            dma((lat_count,)),
+            dma((13,)),
+            dma((lat_count,)),
         ],
         compiler_params=pltpu.CompilerParams(
             collective_id=0, has_side_effects=True, vmem_limit_bytes=63 * 1024 * 1024

time: 46.1 us -> 47.1 us (1.022)
  Pallas kernels: 42.3 us -> 43.3 us
    pallas_call x1, Pallas kernels: 42.3 us -> 43.3 us  [fused_device(): pl.pallas_call(lambda *refs: fused_kernel(nx, nz, *refs), out_shape=jax.S...]
where the time goes in v3:
time: 47.1 us; the launch traced here: 46.9 us
  Pallas kernels  43.3 us (92%)
  between operations  1.95 us (4%)
  local copies, waits for them, and re-layouts  1.62 us (3%)
    pallas_call x1, Pallas kernels, fused_device(): pl.pallas_call(lambda *refs: fused_kernel(nx, nz, *refs), out_shape=jax.S...  43.3 us
    unnamed x1, local copies, waits for them, and re-layouts  1.62 us

profile of v3, /device:TPU:9, one launch (start us, length us, event | category | flops | bytes accessed | tf_op | source)
XLA Modules:
  0.0 46.9 jit_solution(13343677205503735559)
XLA Ops:
  1.9 43.3 %shard_map.109 = bf16[128,768]{1,0:T(8,128)(2,1)} custom-call(f32[2,16]{1,0:T(2,128)} %bitcast.9, s32[1]{0:T(128)S(6)} %copy.13.refs_1_, s32[1]{0:T(128)S(6)} %copy.14.refs_2_, s32[1]{0:T(128)S(6)} %copy.15.refs_3_, bf16[128,768]{1,0:T(8,128)(2,1)} %bitcast.6, f32[768]{0:T(1024)} %refs_5_.1, bf16[96,2304]{1,0:T(8,128)(2,1)} %refs_6_.1, ...), custom_call_target="tpu_custom_call" | custom-call | tf_op jit(solution)/shard_map/pallas_call | solution.py:670
  45.3 1.6 %copy.16 = bf16[1,128,768]{2,1,0:T(8,128)(2,1)} copy(bf16[1,128,768]{2,1,0:T(8,128)(2,1)} %bitcast.5) | data formatting | bytes 393216

commit v4 on v3

--- a/solution.py
+++ b/solution.py
@@ -456,7 +456,19 @@
     def norm_block(yy, cc):
         normed[yy, pl.ds(cc * rows, rows), :] = norm_rows(tok[yy, pl.ds(cc * rows, rows), :], gain_a)
 
+    loads[5].wait()
+    o_own(start)
     norm_block(y, c)
+    gather_q.step(1, True)
+    o_step([0])
+    tok_copies[1].wait_recv()
+    norm_block(y, 1 - c)
+    gather_q.step(2, True)
+    tok_copies[0].wait_recv()
+    tok_copies[2].start()
+    o_step(range(1, 5))
+    gather_q.step(3, True)
+    o_step(range(5, 9))
     loads[3].wait()
     pair_row = lax.broadcasted_iota(jnp.int32, (2 * head, width), 0)
     pair_col = lax.broadcasted_iota(jnp.int32, (2 * head, width), 1)
@@ -465,23 +477,13 @@
         wide = jnp.concatenate([w_conv[b], w_conv[b]], axis=0).astype(F32)
         mixer[b] = jnp.where(same, wide, 0.0).astype(BF)
 
-    gather_q.step(1, True)
-    tok_copies[1].wait_recv()
-    norm_block(y, 1 - c)
-    tok_copies[0].wait_recv()
-    tok_copies[2].start()
-    gather_q.step(2, True)
     norm_block(1 - y, c)
-    loads[5].wait()
-    o_own(start)
     tok_copies[2].wait_recv()
     norm_block(1 - y, 1 - c)
-    gather_q.step(3, True)
-    o_step([0])
     tok_copies[3].wait_recv()
     bias_f[...] = jnp.concatenate([bias[0], bias[1]], axis=1).astype(F32)
+    o_step(range(9, 13))
     gather_q.across()
-    o_step(range(1, 5))
 
     def att_copy(r, to_c, k, device):
         return remote(
@@ -512,10 +514,8 @@
     attend(1 - y, 0, lambda: None)
     att_copies[0].start()
     att_copies[1].start()
-    o_step(range(5, 9))
     attend(y, 1, lambda: None)
     att_copies[2].start()
-    o_step(range(9, 13))
     att_in[quad] = att_out[1, pl.ds(c * rows, rows), :]
 
     o_collect()

time: 47.1 us -> 42.3 us (0.90)
  Pallas kernels: 43.3 us -> 38.6 us
    pallas_call x1, Pallas kernels: 43.3 us -> 38.6 us  [fused_device(): pl.pallas_call(lambda *refs: fused_kernel(nx, nz, *refs), out_shape=jax.S...]
where the time goes in v4:
time: 42.3 us; the launch traced here: 42.1 us
  Pallas kernels  38.6 us (91%)
  between operations  1.95 us (5%)
  local copies, waits for them, and re-layouts  1.62 us (4%)
    pallas_call x1, Pallas kernels, fused_device(): pl.pallas_call(lambda *refs: fused_kernel(nx, nz, *refs), out_shape=jax.S...  38.6 us
    unnamed x1, local copies, waits for them, and re-layouts  1.62 us

profile of v4, /device:TPU:9, one launch (start us, length us, event | category | flops | bytes accessed | tf_op | source)
XLA Modules:
  0.0 42.1 jit_solution(14322412447963546469)
XLA Ops:
  1.9 38.6 %shard_map.109 = bf16[128,768]{1,0:T(8,128)(2,1)} custom-call(f32[2,16]{1,0:T(2,128)} %bitcast.9, s32[1]{0:T(128)S(6)} %copy.13.refs_1_, s32[1]{0:T(128)S(6)} %copy.14.refs_2_, s32[1]{0:T(128)S(6)} %copy.15.refs_3_, bf16[128,768]{1,0:T(8,128)(2,1)} %bitcast.6, f32[768]{0:T(1024)} %refs_5_.1, bf16[96,2304]{1,0:T(8,128)(2,1)} %refs_6_.1, ...), custom_call_target="tpu_custom_call" | custom-call | tf_op jit(solution)/shard_map/pallas_call | solution.py:670
  40.5 1.6 %copy.16 = bf16[1,128,768]{2,1,0:T(8,128)(2,1)} copy(bf16[1,128,768]{2,1,0:T(8,128)(2,1)} %bitcast.5) | data formatting | bytes 393216
